TPU v7x, 256 devices: a whole 4x4x8 slice. The times are simulated.
256 devices in a mesh: shard: 64 (over y, z, core), tensor: 4 (over x).
Axes of the slice: x: 4, y: 4, z: 8, core: 2. Of those that a mesh axis runs over, the one named last changes fastest.
Arguments:
- gradient: bfloat16 [64, 1024, 1024], P(None, 'shard', 'tensor'), may hold values from -64 to 64, as said below
- momentum: float32 [64, 1024, 1024], P(None, 'shard', 'tensor'), may hold values from -64 to 64, as said below
Outputs:
- momentum_out: float32 [64, 1024, 1024], P(None, 'shard', 'tensor')
- update: float32 [64, 1024, 1024], P(None, 'shard', 'tensor')
Inputs may be any that keep to these rules, and one draw needn't show every extreme that they name: `gradient`: finite real values. `momentum`: finite real values.
All inputs are finite; a program needn't handle non-finite values.
Results may differ from a plain program's by a relative error of at most 0.0003.
Values sent between devices are 32-bit elements; how exact they have to be, the bound alone decides.
No kernel may reach another device: no remote copies, remote signals or barrier semaphores. Data moves between devices by JAX's collectives and lax.ppermute only.
A program may use at most 64 MiB of HBM per device.

v0:
```python
import math

import jax
import jax.numpy as jnp
from jax import lax
from jax.sharding import PartitionSpec as P

D = 1024
BLOCK = 1024
ITERS = 3


first_coef = 3.4445
second_coef = -4.775
third_coef = 2.0315
decay_rate = 0.95


def product(left, right):
    return jnp.einsum(
        "ij,jl->il",
        left,
        right,
        precision=lax.Precision.HIGHEST,
        preferred_element_type=jnp.float32,
    )


def against(left, right):
    return jnp.einsum(
        "ij,lj->il",
        left,
        right,
        precision=lax.Precision.HIGHEST,
        preferred_element_type=jnp.float32,
    )


def per_device(gradient, momentum):
    widened = gradient.astype(jnp.float32)
    momentum_out = decay_rate * momentum + widened
    direction = widened + decay_rate * momentum_out
    by_owner = lax.all_to_all(direction, "shard", split_axis=0, concat_axis=0, tiled=True)
    row_pieces = lax.all_to_all(by_owner, "tensor", split_axis=1, concat_axis=2, tiled=True)
    piece_count = row_pieces.shape[0]
    piece_rows = row_pieces.shape[1]
    width = row_pieces.shape[2]
    iterate = row_pieces.reshape(piece_count * piece_rows, width)
    norm_total = lax.psum(jnp.sum(iterate * iterate), "tensor")
    iterate = iterate / (jnp.sqrt(norm_total) + 1e-07)
    for sweep_index in range(ITERS):
        full_rows = lax.all_gather(iterate, "tensor", axis=0, tiled=True)
        gram_rows = against(iterate, full_rows)
        full_gram = lax.all_gather(gram_rows, "tensor", axis=0, tiled=True)
        square_rows = product(gram_rows, full_gram)
        polynomial = second_coef * gram_rows + third_coef * square_rows
        iterate = first_coef * iterate + product(polynomial, full_rows)
    result = (0.2 * math.sqrt(max(BLOCK, D)) * iterate).reshape(piece_count, piece_rows, width)
    update = lax.all_to_all(
        lax.all_to_all(result, "shard", split_axis=0, concat_axis=0, tiled=True),
        "tensor",
        split_axis=2,
        concat_axis=1,
        tiled=True,
    )
    return (momentum_out, update)


def solution(mesh):
    placed = (P(None, "shard", "tensor"), P(None, "shard", "tensor"))
    return jax.shard_map(
        per_device,
        mesh=mesh,
        in_specs=placed,
        out_specs=(P(None, "shard", "tensor"), P(None, "shard", "tensor")),
        check_vma=False,
    )
```

profile of v0, /device:TPU:1, one launch (start us, length us, event | category | flops | bytes accessed | tf_op | source)
XLA Modules:
  0.0 516.6 jit_solution(14466420875342971486)
XLA Ops:
  7.2 2.6 convert_add_fusion
  9.8 41.5 %all_to_all.37 = f32[64,16,256]{2,1,0:T(8,128)S(1)} all-to-all(f32[64,16,256]{2,1,0:T(8,128)S(1)} %get-tuple-element.4), channel_id=1, replica_groups=mesh['shard'=64,'tensor'=4] {'shard'}, dimensions={0} | all-to-all | bytes 2097152 | tf_op jit(solution)/shard_map/all_to_all | solution.py:43
  51.8 18.7 %all_to_all.38 = f32[64,16,256]{2,0,1:T(8,128)S(1)} all-to-all(f32[64,16,256]{2,0,1:T(8,128)S(1)} %copy.12), channel_id=1, replica_groups=mesh['shard'=64,'tensor'=4] {'tensor'}, dimensions={1} | all-to-all | bytes 2097152 | tf_op jit(solution)/shard_map/all_to_all | solution.py:44
  71.4 7.6 %psum.7 = f32[]{:T(128)} all-reduce(f32[]{:T(128)} %multiply_reduce_fusion), channel_id=1, replica_groups=mesh['shard'=64,'tensor'=4] {'tensor'}, use_global_device_ids=true, to_apply=%region_1.0 | all-reduce | flops 1 | bytes 8 | tf_op jit(solution)/shard_map/psum | solution.py:49
  81.6 47.9 %all-gather.7.cloned.1.call-done = f32[1024,1024]{1,0:T(8,128)} async-done(((f32[256,1024]{1,0:T(8,128)}), f32[1024,1024]{1,0:T(8,128)}) %all-gather.7.cloned.1.call-update) | async-done | bytes 4194320 | tf_op jit(solution)/shard_map/all_gather | solution.py:52
  129.6 7.3 %fusion.4 = f32[256,1024]{1,0:T(8,128)} fusion(f32[256,1024]{1,0:T(8,128)} %bitcast.29, f32[1024,1024]{1,0:T(8,128)} %all-gather.7.cloned.1.call-done), kind=kOutput, calls=%fused_computation.14 | convolution fusion | flops 3221225472 | bytes 6291456 | tf_op jit(solution)/shard_map/ij,lj->il/dot_general | solution.py:30
  137.4 50.7 %all-gather.9.cloned.1.call-done = f32[1024,1024]{1,0:T(8,128)} async-done(((f32[256,1024]{1,0:T(8,128)}), f32[1024,1024]{1,0:T(8,128)}) %all-gather.9.cloned.1.call-update) | async-done | bytes 4194320 | tf_op jit(solution)/shard_map/all_gather | solution.py:54
  188.1 6.7 %fusion.3 = f32[256,1024]{1,0:T(8,128)S(1)} fusion(f32[256,1024]{1,0:T(8,128)} %fusion.4, f32[1024,1024]{1,0:T(8,128)} %all-gather.9.cloned.1.call-done), kind=kOutput, calls=%fused_computation.9 | convolution fusion | flops 3222011904 | bytes 6291456 | tf_op jit(solution)/shard_map/ij,jl->il/dot_general | solution.py:20
  194.8 4.7 convolution_add_fusion.2
  199.6 51.2 %all-gather.11.cloned.1.call-done = f32[1024,1024]{1,0:T(8,128)} async-done(((f32[256,1024]{1,0:T(8,128)}), f32[1024,1024]{1,0:T(8,128)}) %all-gather.11.cloned.1.call-update) | async-done | bytes 4194320 | tf_op jit(solution)/shard_map/all_gather | solution.py:52
  250.8 7.3 %fusion.5 = f32[256,1024]{1,0:T(8,128)} fusion(f32[256,1024]{1,0:T(8,128)} %convolution_add_fusion.2, f32[1024,1024]{1,0:T(8,128)} %all-gather.11.cloned.1.call-done), kind=kOutput, calls=%fused_computation.15 | convolution fusion | flops 3221225472 | bytes 6291456 | tf_op jit(solution)/shard_map/ij,lj->il/dot_general | solution.py:30
  258.3 51.0 %all-gather.13.cloned.1.call-done = f32[1024,1024]{1,0:T(8,128)} async-done(((f32[256,1024]{1,0:T(8,128)}), f32[1024,1024]{1,0:T(8,128)}) %all-gather.13.cloned.1.call-update) | async-done | bytes 4194320 | tf_op jit(solution)/shard_map/all_gather | solution.py:54
  309.4 6.7 %fusion.2 = f32[256,1024]{1,0:T(8,128)S(1)} fusion(f32[256,1024]{1,0:T(8,128)} %fusion.5, f32[1024,1024]{1,0:T(8,128)} %all-gather.13.cloned.1.call-done), kind=kOutput, calls=%fused_computation.6 | convolution fusion | flops 3222011904 | bytes 6291456 | tf_op jit(solution)/shard_map/ij,jl->il/dot_general | solution.py:20
  316.1 4.7 convolution_add_fusion.1
  321.1 51.0 %all-gather.15.cloned.1.call-done = f32[1024,1024]{1,0:T(8,128)} async-done(((f32[256,1024]{1,0:T(8,128)}), f32[1024,1024]{1,0:T(8,128)}) %all-gather.15.cloned.1.call-update) | async-done | bytes 4194320 | tf_op jit(solution)/shard_map/all_gather | solution.py:52
  372.1 7.3 %fusion.6 = f32[256,1024]{1,0:T(8,128)} fusion(f32[256,1024]{1,0:T(8,128)} %convolution_add_fusion.1, f32[1024,1024]{1,0:T(8,128)} %all-gather.15.cloned.1.call-done), kind=kOutput, calls=%fused_computation.16 | convolution fusion | flops 3221225472 | bytes 6291456 | tf_op jit(solution)/shard_map/ij,lj->il/dot_general | solution.py:30
  379.4 51.3 %all-gather.17.cloned.1.call-done = f32[1024,1024]{1,0:T(8,128)} async-done(((f32[256,1024]{1,0:T(8,128)}), f32[1024,1024]{1,0:T(8,128)}) %all-gather.17.cloned.1.call-update) | async-done | bytes 4194320 | tf_op jit(solution)/shard_map/all_gather | solution.py:54
  430.6 6.7 %fusion.1 = f32[256,1024]{1,0:T(8,128)S(1)} fusion(f32[256,1024]{1,0:T(8,128)} %fusion.6, f32[1024,1024]{1,0:T(8,128)} %all-gather.17.cloned.1.call-done), kind=kOutput, calls=%fused_computation.3 | convolution fusion | flops 3222011904 | bytes 6291456 | tf_op jit(solution)/shard_map/ij,jl->il/dot_general | solution.py:20
  437.3 3.8 fusion
  441.4 39.4 %all_to_all.39 = f32[64,4,1024]{2,1,0:T(4,128)S(1)} all-to-all(f32[64,4,1024]{2,1,0:T(4,128)S(1)} %reshape.14), channel_id=1, replica_groups=mesh['shard'=64,'tensor'=4] {'shard'}, dimensions={0} | all-to-all | bytes 2097152 | tf_op jit(solution)/shard_map/all_to_all | solution.py:60
  481.7 2.0 reshape.15
  483.8 17.7 %all_to_all.40 = f32[4,1,65536]{2,1,0:T(1,128)S(1)} all-to-all(f32[4,1,65536]{2,1,0:T(1,128)S(1)} %reshape.15), channel_id=1, replica_groups=mesh['shard'=64,'tensor'=4] {'tensor'}, dimensions={0} | all-to-all | bytes 2097152 | tf_op jit(solution)/shard_map/all_to_all | solution.py:59
  502.0 3.7 reduce.3
  505.7 1.4 reshape.16
  (34 shorter events, 8.8 us)
Async XLA Ops:
  7.2 122.4 %all-gather.7.cloned.1.call-start = ((), (), s32[]{:S(2)}) async-start(), calls=%async_computation.4 | async-start | bytes 5242880 | tf_op jit(solution)/shard_map/all_gather | solution.py:52
  81.6 106.5 %all-gather.9.cloned.1.call-start = ((), (), s32[]{:S(2)}) async-start(), calls=%async_computation.5 | async-start | bytes 5242880 | tf_op jit(solution)/shard_map/all_gather | solution.py:54
  136.8 58.0 %copy-start.5 = (f32[32,8,4,256]{3,1,2,0:T(8,128)S(1)}, f32[32,8,4,256]{3,1,2,0:T(8,128)}, u32[]{:S(2)}) copy-start(f32[32,8,4,256]{3,1,2,0:T(8,128)} %copy.16) | copy-start | bytes 3145732
  136.9 114.0 %all-gather.11.cloned.1.call-start = ((), (), s32[]{:S(2)}) async-start(), calls=%async_computation.6 | async-start | bytes 5242880 | tf_op jit(solution)/shard_map/all_gather | solution.py:52
  188.1 6.7 %copy-start = (f32[1024,1024]{1,0:T(8,128)S(1)}, f32[1024,1024]{1,0:T(8,128)}, u32[]{:S(2)}) copy-start(f32[1024,1024]{1,0:T(8,128)} %all-gather.7.cloned.1.call-done) | copy-start | bytes 12582916
  199.6 109.8 %all-gather.13.cloned.1.call-start = ((), (), s32[]{:S(2)}) async-start(), calls=%async_computation.7 | async-start | bytes 5242880 | tf_op jit(solution)/shard_map/all_gather | solution.py:54
  258.1 58.0 %copy-start.3 = (f32[256,1024]{1,0:T(8,128)S(1)}, f32[256,1024]{1,0:T(8,128)}, u32[]{:S(2)}) copy-start(f32[256,1024]{1,0:T(8,128)} %convolution_add_fusion.2) | copy-start | bytes 3145732
  258.1 114.0 %all-gather.15.cloned.1.call-start = ((), (), s32[]{:S(2)}) async-start(), calls=%async_computation.8 | async-start | bytes 5242880 | tf_op jit(solution)/shard_map/all_gather | solution.py:52
  309.4 6.7 %copy-start.1 = (f32[1024,1024]{1,0:T(8,128)S(1)}, f32[1024,1024]{1,0:T(8,128)}, u32[]{:S(2)}) copy-start(f32[1024,1024]{1,0:T(8,128)} %all-gather.11.cloned.1.call-done) | copy-start | bytes 12582916
  320.8 109.8 %all-gather.17.cloned.1.call-start = ((), (), s32[]{:S(2)}) async-start(), calls=%async_computation.9 | async-start | bytes 5242880 | tf_op jit(solution)/shard_map/all_gather | solution.py:54
  379.3 58.0 %copy-start.4 = (f32[256,1024]{1,0:T(8,128)S(1)}, f32[256,1024]{1,0:T(8,128)}, u32[]{:S(2)}) copy-start(f32[256,1024]{1,0:T(8,128)} %convolution_add_fusion.1) | copy-start | bytes 3145732
  430.6 6.7 %copy-start.2 = (f32[1024,1024]{1,0:T(8,128)S(1)}, f32[1024,1024]{1,0:T(8,128)}, u32[]{:S(2)}) copy-start(f32[1024,1024]{1,0:T(8,128)} %all-gather.15.cloned.1.call-done) | copy-start | bytes 12582916
Sparse Core Ops, SparseCore 0:
  81.7 47.8 all-gather.6
  137.0 51.0 all-gather.8
  199.7 51.0 all-gather.10
  258.2 51.0 all-gather.12
  320.9 51.0 all-gather.14
  379.5 51.0 all-gather.16
where the time goes:
time: 522 us; the launch traced here: 517 us
  waiting for transfers between devices  303 us (58%)
  blocking collectives  125 us (24%)
  matrix products  55 us (11%)
  between operations  15.2 us (3%)
  local copies, waits for them, and re-layouts  10 us (2%)
  other arithmetic  7.21 us (1%)
    all_gather x3, waiting for transfers between devices, per_device(): full_gram = lax.all_gather(gram_rows, 'tensor', axis=0, tiled=True)  153 us
    all_gather x3, waiting for transfers between devices, per_device(): full_rows = lax.all_gather(iterate, 'tensor', axis=0, tiled=True)  150 us
    all_to_all x1, blocking collectives, per_device(): lax.all_to_all(direction, 'shard', split_axis=0, concat_axis=0, tiled=True)  41.5 us
    all_to_all x1, blocking collectives, per_device(): lax.all_to_all(result, 'shard', split_axis=0, concat_axis=0, tiled=True)  39.4 us
    dot_general x6, matrix products, product(): jnp.einsum('ij,jl->il', left, right, precision=lax.Precision.HIGHEST, pre...  33.2 us
    dot_general x3, matrix products, against(): jnp.einsum('ij,lj->il', left, right, precision=lax.Precision.HIGHEST, pre...  21.8 us
    all_to_all x1, blocking collectives, per_device(): lax.all_to_all(by_owner, 'tensor', split_axis=1, concat_axis=2, tiled=True)  18.7 us
    all_to_all x1, blocking collectives, per_device(): lax.all_to_all(lax.all_to_all(result, 'shard', split_axis=0, concat_axis=...  17.7 us
  transfers between devices with their start and end apart: 6, of which 6 were waited for; matrix products, arithmetic and copies ran while one was open for 0% of the time, Pallas kernels for 0%

commit v1 on v0

v1 whole, which is shorter than its diff:
```python
import functools
import math

import jax
import jax.numpy as jnp
from jax import lax
from jax.experimental import pallas as pl
from jax.experimental.pallas import tpu as pltpu
from jax.sharding import PartitionSpec as P

D = 1024
BLOCK = 1024
ITERS = 3
HALF = 512
TILE = 256

first_coef = 3.4445
second_coef = -4.775
third_coef = 2.0315
decay_rate = 0.95
out_scale = 0.2 * math.sqrt(max(BLOCK, D))

BY_ROWS = (((1,), (1,)), ((), ()))
BY_COLUMNS = (((1,), (0,)), ((), ()))

HOLDER = (
    ((0, 0, 0), (0, 1, 0), (1, 0, 0), (0, 1, 1)),
    ((0, 0, 1), (1, 1, 1), (1, 0, 1), (1, 1, 0)),
)
SIDE_TO_HOME = (((1, 0), (0, 0)), ((3, 0), (0, 1)), ((3, 1), (2, 0)), ((1, 1), (2, 1)))


def momentum_kernel(gradient_ref, momentum_ref, momentum_out_ref, send_ref):
    widened = gradient_ref[...].astype(jnp.float32)
    momentum_out = decay_rate * momentum_ref[...] + widened
    momentum_out_ref[...] = momentum_out
    direction = widened + decay_rate * momentum_out
    for line in range(direction.shape[0] // 2):
        for core in range(2):
            for tensor in range(4):
                which, rh, ch = HOLDER[core][tensor]
                send_ref[line * 8 + core * 4 + tensor] = direction[
                    line * 2 + which, rh * 8 : rh * 8 + 8, ch * 128 : ch * 128 + 128
                ]


def place_kernel(tiles_ref, update_ref):
    for line in range(update_ref.shape[0] // 2):
        for core in range(2):
            for tensor in range(4):
                which, rh, ch = HOLDER[core][tensor]
                update_ref[line * 2 + which, rh * 8 : rh * 8 + 8, ch * 128 : ch * 128 + 128] = tiles_ref[
                    line * 8 + core * 4 + tensor
                ]


def split(value):
    high = value.astype(jnp.bfloat16)
    return high, (value - high.astype(jnp.float32)).astype(jnp.bfloat16)


def product(left, right, dims):
    dot = functools.partial(lax.dot_general, dimension_numbers=dims, preferred_element_type=jnp.float32)
    return dot(left[0], right[0]) + (dot(left[0], right[1]) + dot(left[1], right[0]))


def rows(index):
    return pl.ds(pl.multiple_of(index * TILE, TILE), TILE)


def newton_schulz_kernel(own_top, own_bottom, other_top, other_bottom, out_top, out_bottom, *scratch):
    first, second, gram, poly = (scratch[i : i + 2] for i in (0, 2, 4, 6))
    count = BLOCK // TILE

    squares = jnp.float32(0)
    for r, c, piece in ((0, 0, own_top), (HALF, 0, own_bottom), (0, HALF, other_top), (HALF, HALF, other_bottom)):

        def load(index, total, r=r, c=c, piece=piece):
            value = piece[rows(index), :]
            high, low = split(value)
            place = pl.ds(pl.multiple_of(r + index * TILE, TILE), TILE)
            first[0][place, c : c + HALF] = high
            first[1][place, c : c + HALF] = low
            return total + jnp.sum(value * value)

        squares = lax.fori_loop(0, HALF // TILE, load, squares)
    inverse = 1.0 / (jnp.sqrt(squares) + 1e-07)

    def symmetric(source, target, finish):
        def outer(i, carry):
            def inner(j, carry):
                left = tuple(part[rows(i), :] for part in source)
                right = tuple(part[rows(j), :] for part in source)
                value = finish(product(left, right, BY_ROWS), i, j)
                target[0][rows(i), rows(j)], target[1][rows(i), rows(j)] = split(value)

                @pl.when(i != j)
                def _():
                    target[0][rows(j), rows(i)], target[1][rows(j), rows(i)] = split(value.T)

                return carry

            return lax.fori_loop(0, i + 1, inner, carry)

        lax.fori_loop(0, count, outer, 0)

    for sweep_index in range(ITERS):
        source, target = ((first, second), (second, first))[sweep_index % 2]
        last = sweep_index == ITERS - 1
        scale = inverse if sweep_index == 0 else jnp.float32(1)
        symmetric(source, gram, lambda value, i, j: value * (scale * scale))

        def polynomial(value, i, j):
            gram_tile = gram[0][rows(i), rows(j)].astype(jnp.float32) + gram[1][rows(i), rows(j)].astype(jnp.float32)
            row = lax.broadcasted_iota(jnp.int32, value.shape, 0)
            column = lax.broadcasted_iota(jnp.int32, value.shape, 1)
            diagonal = jnp.where((row == column) & (i == j), jnp.float32(first_coef), jnp.float32(0))
            return (diagonal + (second_coef * gram_tile + third_coef * value)) * scale

        symmetric(gram, poly, polynomial)

        def apply(i, carry):
            left = tuple(part[rows(i), :] for part in poly)

            def inner(j, carry):
                right = tuple(part[:, rows(j)] for part in source)
                value = product(left, right, BY_COLUMNS)
                if not last:
                    target[0][rows(i), rows(j)], target[1][rows(i), rows(j)] = split(value)
                else:

                    @pl.when(i < count // 2)
                    def _():
                        out_top[rows(i), rows(j)] = out_scale * value

                    @pl.when(i >= count // 2)
                    def _():
                        out_bottom[rows(i - count // 2), rows(j)] = out_scale * value

                return carry

            return lax.fori_loop(0, HALF // TILE if last else count, inner, carry)

        lax.fori_loop(0, count, apply, 0)


def newton_schulz(*pieces):
    in_vmem = pl.BlockSpec(memory_space=pltpu.VMEM)
    return pl.pallas_call(
        newton_schulz_kernel,
        out_shape=[jax.ShapeDtypeStruct((HALF, HALF), jnp.float32)] * 2,
        in_specs=[in_vmem] * 4,
        out_specs=[in_vmem] * 2,
        scratch_shapes=[pltpu.VMEM((BLOCK, BLOCK), jnp.bfloat16)] * 8,
        compiler_params=pltpu.CompilerParams(vmem_limit_bytes=40 * 1024 * 1024),
        name="newton_schulz",
    )(*pieces)


def from_tiles(tiles):
    return tiles.reshape(64, 4, 8, 128).transpose(0, 2, 1, 3).reshape(HALF, HALF)


def to_tiles(quarter):
    return quarter.reshape(64, 8, 4, 128).transpose(0, 2, 1, 3).reshape(256, 8, 128)


def per_device(gradient, momentum):
    axes = ("shard", "tensor")
    lines = 32

    def device(p, place):
        tensor, core = place
        return (2 * p + core) * 4 + tensor

    inward = [(device(p, side), device(p, home)) for p in range(lines) for side, home in SIDE_TO_HOME]
    outward = [(home, side) for side, home in inward]
    swap = [(device(p, (t, c)), device(p, (t, 1 - c))) for p in range(lines) for t in (0, 2) for c in (0, 1)]

    step = 8
    blocked = pl.BlockSpec((step, 16, 256), lambda i: (i, 0, 0))
    tiled = pl.BlockSpec((step * 4, 8, 128), lambda i: (i, 0, 0))
    momentum_out, send = pl.pallas_call(
        momentum_kernel,
        grid=(64 // step,),
        out_shape=[
            jax.ShapeDtypeStruct((64, 16, 256), jnp.float32),
            jax.ShapeDtypeStruct((256, 8, 128), jnp.float32),
        ],
        in_specs=[blocked, blocked],
        out_specs=[blocked, tiled],
        name="momentum",
    )(gradient, momentum)

    own_top = from_tiles(lax.all_to_all(send, axes, split_axis=0, concat_axis=0, tiled=True))
    own_bottom = lax.ppermute(own_top, axes, inward)
    other_top = lax.ppermute(own_top, axes, swap)
    other_bottom = lax.ppermute(own_bottom, axes, swap)
    out_top, out_bottom = newton_schulz(own_top, own_bottom, other_top, other_bottom)
    is_home = (lax.axis_index("tensor") & 1) == 0
    result = jnp.where(is_home, out_top, lax.ppermute(out_bottom, axes, outward))
    tiles = lax.all_to_all(to_tiles(result), axes, split_axis=0, concat_axis=0, tiled=True)
    update = pl.pallas_call(
        place_kernel,
        grid=(64 // step,),
        out_shape=jax.ShapeDtypeStruct((64, 16, 256), jnp.float32),
        in_specs=[tiled],
        out_specs=blocked,
        name="place",
    )(tiles)
    return (momentum_out, update)


def solution(mesh):
    placed = (P(None, "shard", "tensor"), P(None, "shard", "tensor"))
    return jax.shard_map(
        per_device,
        mesh=mesh,
        in_specs=placed,
        out_specs=placed,
        check_vma=False,
    )
```

time: 522 us -> 205 us (0.39)
  waiting for transfers between devices: 303 us -> 27.4 us
  Pallas kernels: 0 us -> 81.3 us
  matrix products: 55 us -> 0 us
  blocking collectives: 125 us -> 87.4 us
  between operations: 15.2 us -> 0.69 us
  local copies, waits for them, and re-layouts: 10 us -> 0 us
  other arithmetic: 7.21 us -> 0.21 us
  starting transfers between devices: 1.16 us -> 7.49 us
    all_gather x6 -> x0, waiting for transfers between devices: 303 us -> none  [the longest x3 153 us: per_device(): full_gram = lax.all_gather(gram_rows, 'tensor', axis=0, tiled=True)]
    pallas_call x0 -> x3, Pallas kernels: none -> 81.3 us  [the longest x1 70.5 us: newton_schulz(): pl.pallas_call(newton_schulz_kernel, out_shape=[jax.ShapeDtypeStruct((HAL...]
    dot_general x9 -> x0, matrix products: 55 us -> none  [the longest x6 33.2 us: product(): jnp.einsum('ij,jl->il', left, right, precision=lax.Precision.HIGHEST, pre...]
    all_to_all x4 -> x2, blocking collectives: 117 us -> 87.4 us  [the longest x1 48.1 us: per_device(): lax.all_to_all(send, axes, split_axis=0, concat_axis=0, tiled=True)]
    ppermute x0 -> x4, waiting for transfers between devices: none -> 27.4 us  [the longest x1 13.3 us: per_device(): own_bottom = lax.ppermute(own_top, axes, inward)]
    psum x1 -> x0, blocking collectives: 7.56 us -> none  [per_device(): norm_total = lax.psum(jnp.sum(iterate * iterate), 'tensor')]
    ppermute x0 -> x4, starting transfers between devices: none -> 7.49 us  [the longest x1 2.75 us: per_device(): other_top = lax.ppermute(own_top, axes, swap)]
  transfers between devices with their start and end apart: 6 -> 4, of which waited for: 6 -> 3; matrix products, arithmetic and copies ran while one was open for 0% -> 0% of each run, Pallas kernels for 0% -> 0%
where the time goes in v1:
time: 205 us; the launch traced here: 204 us
  blocking collectives  87.4 us (43%)
  Pallas kernels  81.3 us (40%)
  waiting for transfers between devices  27.4 us (13%)
  starting transfers between devices  7.49 us (4%)
    pallas_call x1, Pallas kernels, newton_schulz(): pl.pallas_call(newton_schulz_kernel, out_shape=[jax.ShapeDtypeStruct((HAL...  70.5 us
    all_to_all x1, blocking collectives, per_device(): lax.all_to_all(send, axes, split_axis=0, concat_axis=0, tiled=True)  48.1 us
    all_to_all x1, blocking collectives, per_device(): lax.all_to_all(to_tiles(result), axes, split_axis=0, concat_axis=0, tiled...  39.3 us
    ppermute x1, waiting for transfers between devices, per_device(): own_bottom = lax.ppermute(own_top, axes, inward)  13.3 us
    ppermute x1, waiting for transfers between devices, per_device(): lax.ppermute(out_bottom, axes, outward)  11.7 us
    pallas_call x1, Pallas kernels, per_device(): pl.pallas_call(momentum_kernel, grid=(64 // step,), out_shape=[jax.ShapeD...  5.6 us
    pallas_call x1, Pallas kernels, per_device(): pl.pallas_call(place_kernel, grid=(64 // step,), out_shape=jax.ShapeDtype...  5.16 us
  transfers between devices with their start and end apart: 4, of which 3 were waited for; matrix products, arithmetic and copies ran while one was open for 0% of the time, Pallas kernels for 0%

profile of v1, /device:TPU:1, one launch (start us, length us, event | category | flops | bytes accessed | tf_op | source)
XLA Modules:
  0.0 204.4 jit_solution(3064553493000391840)
XLA Ops:
  0.6 5.6 %momentum.1 = (f32[64,16,256]{2,1,0:T(8,128)}, f32[256,8,128]{2,1,0:T(8,128)}) custom-call(bf16[64,16,256]{2,1,0:T(8,128)(2,1)} %gradient_ref.1, f32[64,16,256]{2,1,0:T(8,128)} %momentum_ref.1), custom_call_target="tpu_custom_call" | custom-call | tf_op jit(solution)/shard_map/momentum/pallas_call | solution.py:183
  6.2 48.1 %all_to_all.10 = f32[256,8,128]{2,1,0:T(8,128)S(1)} all-to-all(f32[256,8,128]{2,1,0:T(8,128)} %get-tuple-element.7), channel_id=1, replica_groups=mesh['shard'=64,'tensor'=4] {'shard','tensor'}, dimensions={0} | all-to-all | bytes 2097152 | tf_op jit(solution)/shard_map/all_to_all | solution.py:195
  54.3 1.3 collective-permute-start
  55.6 2.7 %collective-permute-start.1 = (f32[512,512]{1,0:T(8,128)S(1)}, f32[512,512]{1,0:T(8,128)S(1)}, u32[]{:S(2)}, u32[]{:S(2)}) collective-permute-start(f32[512,512]{1,0:T(8,128)S(1)} %bitcast.11), channel_id=1, source_target_pairs={{0,4},{4,0},{2,6},{6,2},{8,12},{12,8},{10,14},{14,10},{16,20},{20,... | collective-permute-start | bytes 3145736 | tf_op jit(solution)/shard_map/ppermute | solution.py:197
  58.4 13.3 %collective-permute-done.own_bottom = f32[512,512]{1,0:T(8,128)S(1)} collective-permute-done((f32[512,512]{1,0:T(8,128)S(1)}, f32[512,512]{1,0:T(8,128)S(1)}, u32[]{:S(2)}, u32[]{:S(2)}) %collective-permute-start) | collective-permute-done | bytes 1048608 | tf_op jit(solution)/shard_map/ppermute | solution.py:196
  71.6 2.1 %collective-permute-start.2 = (f32[512,512]{1,0:T(8,128)S(1)}, f32[512,512]{1,0:T(8,128)S(1)}, u32[]{:S(2)}, u32[]{:S(2)}) collective-permute-start(f32[512,512]{1,0:T(8,128)S(1)} %collective-permute-done.own_bottom), channel_id=1, source_target_pairs={{0,4},{4,0},{2,6},{6,2},{8,12},{12,8},{10,14},{14,10},{16,20},{20,... | collective-permute-start | bytes 3145736 | tf_op jit(solution)/shard_map/ppermute | solution.py:198
  73.7 0.0 collective-permute-done.1.other_top
  73.7 2.4 %collective-permute-done.2.other_bottom = f32[512,512]{1,0:T(8,128)S(1)} collective-permute-done((f32[512,512]{1,0:T(8,128)S(1)}, f32[512,512]{1,0:T(8,128)S(1)}, u32[]{:S(2)}, u32[]{:S(2)}) %collective-permute-start.2) | collective-permute-done | bytes 1048608 | tf_op jit(solution)/shard_map/ppermute | solution.py:198
  76.2 70.5 %newton_schulz.1 = (f32[512,512]{1,0:T(8,128)S(1)}, f32[512,512]{1,0:T(8,128)S(1)}) custom-call(f32[512,512]{1,0:T(8,128)S(1)} %bitcast.12, f32[512,512]{1,0:T(8,128)S(1)} %collective-permute-done.own_bottom, f32[512,512]{1,0:T(8,128)S(1)} %collective-permute-done.1.other_top, f32[512,512]{1,0:T(8,128)S(1)} %collective-permute-done.2.other_bottom), custom_call_target="tpu_custom_call" | custom-call | tf_op jit(solution)/shard_map/newton_schulz/pallas_call | solution.py:149
  146.7 1.4 collective-permute-start.3
  148.1 11.7 %collective-permute-done.3 = f32[512,512]{1,0:T(8,128)S(1)} collective-permute-done((f32[512,512]{1,0:T(8,128)S(1)}, f32[512,512]{1,0:T(8,128)S(1)}, u32[]{:S(2)}, u32[]{:S(2)}) %collective-permute-start.3) | collective-permute-done | bytes 1048608 | tf_op jit(solution)/shard_map/ppermute | solution.py:201
  159.7 0.2 broadcast_select_fusion
  159.9 39.3 %all_to_all.11.tiles_ref = f32[256,8,128]{2,1,0:T(8,128)} all-to-all(f32[256,8,128]{2,1,0:T(8,128)S(1)} %bitcast.13), channel_id=1, replica_groups=mesh['shard'=64,'tensor'=4] {'shard','tensor'}, dimensions={0} | all-to-all | bytes 2097152 | tf_op jit(solution)/shard_map/all_to_all | solution.py:202
  199.3 5.2 %place.1 = f32[64,16,256]{2,1,0:T(8,128)} custom-call(f32[256,8,128]{2,1,0:T(8,128)} %all_to_all.11.tiles_ref), custom_call_target="tpu_custom_call" | custom-call | tf_op jit(solution)/shard_map/place/pallas_call | solution.py:203
Async XLA Ops:
  54.3 17.3 %collective-permute-start = (f32[512,512]{1,0:T(8,128)S(1)}, f32[512,512]{1,0:T(8,128)S(1)}, u32[]{:S(2)}, u32[]{:S(2)}) collective-permute-start(f32[512,512]{1,0:T(8,128)S(1)} %bitcast.10), channel_id=1, source_target_pairs={{1,0},{3,4},{7,2},{5,6},{9,8},{11,12},{15,10},{13,14},{17,16},{19,... | collective-permute-start | bytes 3145736 | tf_op jit(solution)/shard_map/ppermute | solution.py:196
  55.6 18.1 %collective-permute-start.1 = (f32[512,512]{1,0:T(8,128)S(1)}, f32[512,512]{1,0:T(8,128)S(1)}, u32[]{:S(2)}, u32[]{:S(2)}) collective-permute-start(f32[512,512]{1,0:T(8,128)S(1)} %bitcast.11), channel_id=1, source_target_pairs={{0,4},{4,0},{2,6},{6,2},{8,12},{12,8},{10,14},{14,10},{16,20},{20,... | collective-permute-start | bytes 3145736 | tf_op jit(solution)/shard_map/ppermute | solution.py:197
  71.6 4.5 %collective-permute-start.2 = (f32[512,512]{1,0:T(8,128)S(1)}, f32[512,512]{1,0:T(8,128)S(1)}, u32[]{:S(2)}, u32[]{:S(2)}) collective-permute-start(f32[512,512]{1,0:T(8,128)S(1)} %collective-permute-done.own_bottom), channel_id=1, source_target_pairs={{0,4},{4,0},{2,6},{6,2},{8,12},{12,8},{10,14},{14,10},{16,20},{20,... | collective-permute-start | bytes 3145736 | tf_op jit(solution)/shard_map/ppermute | solution.py:198
  146.7 13.0 %collective-permute-start.3 = (f32[512,512]{1,0:T(8,128)S(1)}, f32[512,512]{1,0:T(8,128)S(1)}, u32[]{:S(2)}, u32[]{:S(2)}) collective-permute-start(f32[512,512]{1,0:T(8,128)S(1)} %get-tuple-element.9), channel_id=1, source_target_pairs={{0,1},{4,3},{2,7},{6,5},{8,9},{12,11},{10,15},{14,13},{16,17},{20,... | collective-permute-start | bytes 3145736 | tf_op jit(solution)/shard_map/ppermute | solution.py:201

commit v2 on v0

v2 whole, which is shorter than its diff:
```python
import math

import jax
import jax.numpy as jnp
from jax import lax
from jax.experimental import pallas as pl
from jax.experimental.pallas import tpu as pltpu
from jax.sharding import PartitionSpec as P

D = 1024
BLOCK = 1024
ITERS = 3
HALF = 512
TILE = 256

first_coef = 3.4445
second_coef = -4.775
third_coef = 2.0315
decay_rate = 0.95
out_scale = 0.2 * math.sqrt(max(BLOCK, D))

PIECE_ROWS = (512, 176, 176, 160)
PIECE_STARTS = (0, 512, 688, 864)

BY_ROWS = (((1,), (1,)), ((), ()))
BY_COLUMNS = (((1,), (0,)), ((), ()))

SIZES = (4, 4, 8)
LINES = (22, 22, 20)
STARTS = (0, 22, 44)
CHIPS = [(x, y, z) for y in range(4) for z in range(8) for x in range(4)]
HOMES = [chip for chip in CHIPS if sum(chip) % 2 == 0]


def device(chip, core):
    x, y, z = chip
    return ((y * 8 + z) * 2 + core) * 4 + x


def neighbour(chip, axis, step):
    return tuple((c + step) % SIZES[i] if i == axis else c for i, c in enumerate(chip))


def side(chip, core, axis):
    return device(neighbour(chip, axis, 1 if core else -1), core)


def lower_holder(chip, core):
    line = lax.axis_index("shard")
    x, y, z = (side(chip, core, axis) for axis in range(3))
    return jnp.where(line < STARTS[1], x, jnp.where(line < STARTS[2], y, z))


def direction_kernel(gradient_ref, momentum_ref, send_ref):
    for block, chip in enumerate(HOMES):
        widened = gradient_ref[block].astype(jnp.float32)
        direction = widened + decay_rate * (decay_rate * momentum_ref[block] + widened)
        for core in range(2):
            columns = slice(core * 128, core * 128 + 128)
            send_ref[device(chip, core)] = direction[:8, columns]
            send_ref[lower_holder(chip, core)] = direction[8:, columns]


def place_kernel(tiles_ref, update_ref):
    for block, chip in enumerate(HOMES):
        for core in range(2):
            columns = slice(core * 128, core * 128 + 128)
            update_ref[block, :8, columns] = tiles_ref[device(chip, core)]
            update_ref[block, 8:, columns] = tiles_ref[lower_holder(chip, core)]


def split(value):
    high = value.astype(jnp.bfloat16)
    return high, (value - high.astype(jnp.float32)).astype(jnp.bfloat16)


def dot(left, right, dims):
    return lax.dot_general(left, right, dims, preferred_element_type=jnp.float32)


def product(left, right, dims):
    return dot(left[0], right[0], dims) + (dot(left[0], right[1], dims) + dot(left[1], right[0], dims))


def newton_schulz_kernel(*refs):
    pieces, outs, scratch = refs[:4], refs[4:8], refs[8:]
    iterate, gram, poly = (scratch[i : i + 2] for i in (0, 2, 4))
    panels = [slice(i, i + TILE) for i in range(0, BLOCK, TILE)]

    squares = jnp.zeros((16, HALF), jnp.float32)
    for index, piece in enumerate(pieces):
        base, c = (index % 2) * HALF, (index // 2) * HALF
        for r in range(0, HALF, 16):
            value = piece[r : r + 16, :]
            place = slice(base + r, base + r + 16)
            iterate[0][0, place, c : c + HALF], iterate[1][0, place, c : c + HALF] = split(value)
            squares = squares + value * value
    inverse = 1.0 / (jnp.sqrt(jnp.sum(squares)) + 1e-07)

    def symmetric(source, target, finish):
        for i, panel in enumerate(panels):
            high, low = (part[panel, :] for part in source)
            cross = dot(high, low, BY_ROWS)
            value = finish(dot(high, high, BY_ROWS) + (cross + cross.T), panel, panel)
            target[0][panel, panel], target[1][panel, panel] = split(value)
            if i:
                before = slice(0, i * TILE)
                value = finish(product((high, low), tuple(part[before, :] for part in source), BY_ROWS), panel, before)
                target[0][panel, before], target[1][panel, before] = split(value)
                target[0][before, panel], target[1][before, panel] = split(value.T)

    def sweep(sweep_index, carry):
        now = sweep_index & 1
        source = tuple(part.at[now] for part in iterate)
        target = tuple(part.at[1 - now] for part in iterate)
        scale = jnp.where(sweep_index == 0, inverse, jnp.float32(1))
        symmetric(source, gram, lambda value, panel, columns: value * (scale * scale))

        def polynomial(value, panel, columns):
            gram_tile = gram[0][panel, columns].astype(jnp.float32) + gram[1][panel, columns].astype(jnp.float32)
            value = (second_coef * scale) * gram_tile + (third_coef * scale) * value
            if panel == columns:
                row = lax.broadcasted_iota(jnp.int32, value.shape, 0)
                column = lax.broadcasted_iota(jnp.int32, value.shape, 1)
                value = value + jnp.where(row == column, first_coef * scale, jnp.float32(0))
            return value

        symmetric(gram, poly, polynomial)

        def apply(half, carry):
            columns = pl.ds(pl.multiple_of(half * HALF, HALF), HALF)
            right = tuple(part[:, columns] for part in source)
            for panel in panels:
                value = product(tuple(part[panel, :] for part in poly), right, BY_COLUMNS)
                target[0][panel, columns], target[1][panel, columns] = split(value)
                for start, out in zip(PIECE_STARTS, outs):
                    low = max(start, panel.start)
                    high = min(start + out.shape[0], panel.stop)
                    if low < high:
                        out[low - start : high - start, :] = out_scale * value[low - panel.start : high - panel.start]
            return carry

        return lax.fori_loop(0, jnp.where(sweep_index == ITERS - 1, 1, 2), apply, carry)

    lax.fori_loop(0, ITERS, sweep, 0)


def newton_schulz(*pieces):
    in_vmem = pl.BlockSpec(memory_space=pltpu.VMEM)
    return pl.pallas_call(
        newton_schulz_kernel,
        out_shape=[jax.ShapeDtypeStruct((n, HALF), jnp.float32) for n in PIECE_ROWS],
        in_specs=[in_vmem] * 4,
        out_specs=[in_vmem] * 4,
        scratch_shapes=[pltpu.VMEM((2, BLOCK, BLOCK), jnp.bfloat16)] * 2 + [pltpu.VMEM((BLOCK, BLOCK), jnp.bfloat16)] * 4,
        compiler_params=pltpu.CompilerParams(vmem_limit_bytes=40 * 1024 * 1024),
        name="newton_schulz",
    )(*pieces)


def from_tiles(tiles):
    return tiles.reshape(64, 4, 8, 128).transpose(0, 2, 1, 3).reshape(HALF, HALF)


def to_tiles(quarter):
    return quarter.reshape(64, 8, 4, 128).transpose(0, 2, 1, 3).reshape(256, 8, 128)


def per_device(gradient, momentum):
    axes = ("shard", "tensor")
    cores = (0, 1)
    inward = [[(side(chip, core, axis), device(chip, core)) for chip in HOMES for core in cores] for axis in range(3)]
    swap = [(device(chip, core), device(chip, 1 - core)) for chip in HOMES for core in cores]

    whole = pl.BlockSpec(memory_space=pltpu.VMEM)
    small = pltpu.CompilerParams(vmem_limit_bytes=16 * 1024 * 1024)
    send = pl.pallas_call(
        direction_kernel,
        out_shape=jax.ShapeDtypeStruct((256, 8, 128), jnp.float32),
        in_specs=[whole] * 2,
        out_specs=whole,
        compiler_params=small,
        name="direction",
    )(gradient, momentum)
    momentum_out = decay_rate * momentum + gradient.astype(jnp.float32)

    received = from_tiles(lax.all_to_all(send, axes, split_axis=0, concat_axis=0, tiled=True))
    arrived = []
    for pairs, start, count in zip(inward, STARTS, LINES):
        arrived.append(lax.ppermute(received[start * 8 : (start + count) * 8], axes, pairs))
    own = (received, jnp.concatenate(arrived, axis=0))
    other = [lax.ppermute(piece, axes, swap) for piece in own]
    top, *bottom = newton_schulz(*own, *other)
    outward = [[(home, holder) for holder, home in pairs] for pairs in inward]
    passed = jnp.concatenate([lax.ppermute(piece, axes, pairs) for piece, pairs in zip(bottom, outward)], axis=0)
    line = lax.axis_index("shard") >> 1
    is_home = ((lax.axis_index("tensor") + (line >> 3) + line) & 1) == 0
    result = jnp.where(is_home, top, passed)
    tiles = lax.all_to_all(to_tiles(result), axes, split_axis=0, concat_axis=0, tiled=True)
    update = pl.pallas_call(
        place_kernel,
        out_shape=jax.ShapeDtypeStruct((64, 16, 256), jnp.float32),
        in_specs=[whole],
        out_specs=whole,
        compiler_params=small,
        name="place",
    )(tiles)
    return (momentum_out, update)


def solution(mesh):
    placed = (P(None, "shard", "tensor"), P(None, "shard", "tensor"))
    return jax.shard_map(
        per_device,
        mesh=mesh,
        in_specs=placed,
        out_specs=placed,
        check_vma=False,
    )
```

time: 522 us -> 161 us (0.31)
  waiting for transfers between devices: 303 us -> 41.3 us
  blocking collectives: 125 us -> 47.9 us
  matrix products: 55 us -> 0 us
  Pallas kernels: 0 us -> 42.5 us
  starting transfers between devices: 1.16 us -> 23.5 us
  between operations: 15.2 us -> 0.79 us
  local copies, waits for them, and re-layouts: 10 us -> 2.41 us
    all_gather x6 -> x0, waiting for transfers between devices: 303 us -> none  [the longest x3 153 us: per_device(): full_gram = lax.all_gather(gram_rows, 'tensor', axis=0, tiled=True)]
    all_to_all x4 -> x1, blocking collectives: 117 us -> 47.9 us  [per_device(): lax.all_to_all(send, axes, split_axis=0, concat_axis=0, tiled=True)]
    dot_general x9 -> x0, matrix products: 55 us -> none  [the longest x6 33.2 us: product(): jnp.einsum('ij,jl->il', left, right, precision=lax.Precision.HIGHEST, pre...]
    pallas_call x0 -> x3, Pallas kernels: none -> 42.5 us  [the longest x1 41.1 us: newton_schulz(): pl.pallas_call(newton_schulz_kernel, out_shape=[jax.ShapeDtypeStruct((n,...]
    all_to_all x0 -> x1, waiting for transfers between devices: none -> 31.3 us  [per_device(): lax.all_to_all(to_tiles(result), axes, split_axis=0, concat_axis=0, tiled...]
    ppermute x0 -> x8, starting transfers between devices: none -> 15.6 us  [the longest x2 7.74 us: per_device(): other = [lax.ppermute(piece, axes, swap) for piece in own]]
    ppermute x0 -> x8, waiting for transfers between devices: none -> 10.1 us  [the longest x3 4 us: per_device(): lax.ppermute(received[start * 8:(start + count) * 8], axes, pairs)]
    all_to_all x0 -> x1, starting transfers between devices: none -> 7.95 us  [per_device(): lax.all_to_all(to_tiles(result), axes, split_axis=0, concat_axis=0, tiled...]
  transfers between devices with their start and end apart: 6 -> 9, of which waited for: 6 -> 6; matrix products, arithmetic and copies ran while one was open for 0% -> 1% of each run, Pallas kernels for 0% -> 0%
where the time goes in v2:
time: 161 us
  blocking collectives  47.9 us (30%)
  Pallas kernels  42.5 us (26%)
  waiting for transfers between devices  41.3 us (26%)
  starting transfers between devices  23.5 us (15%)
  local copies, waits for them, and re-layouts  2.41 us (1%)
  other arithmetic  2.31 us (1%)
    all_to_all x1, blocking collectives, per_device(): lax.all_to_all(send, axes, split_axis=0, concat_axis=0, tiled=True)  47.9 us
    pallas_call x1, Pallas kernels, newton_schulz(): pl.pallas_call(newton_schulz_kernel, out_shape=[jax.ShapeDtypeStruct((n,...  41.1 us
    all_to_all x1, waiting for transfers between devices, per_device(): lax.all_to_all(to_tiles(result), axes, split_axis=0, concat_axis=0, tiled...  31.3 us
    all_to_all x1, starting transfers between devices, per_device(): lax.all_to_all(to_tiles(result), axes, split_axis=0, concat_axis=0, tiled...  7.95 us
    ppermute x2, starting transfers between devices, per_device(): other = [lax.ppermute(piece, axes, swap) for piece in own]  7.74 us
    ppermute x3, waiting for transfers between devices, per_device(): lax.ppermute(received[start * 8:(start + count) * 8], axes, pairs)  4 us
    ppermute x3, waiting for transfers between devices, per_device(): lax.ppermute(piece, axes, pairs)  3.98 us
    ppermute x3, starting transfers between devices, per_device(): lax.ppermute(piece, axes, pairs)  3.93 us
  transfers between devices with their start and end apart: 9, of which 6 were waited for; matrix products, arithmetic and copies ran while one was open for 1% of the time, Pallas kernels for 0%

profile of v2, /device:TPU:1, one launch (start us, length us, event | category | flops | bytes accessed | tf_op | source)
XLA Modules:
  0.0 160.7 jit_solution(1403822429932766356)
XLA Ops:
  0.6 0.0 copy-start
  0.6 1.2 copy-done
  1.9 1.0 copy-done.2
  2.9 0.2 direction.1
  3.1 47.9 %all_to_all.10 = f32[256,8,128]{2,1,0:T(8,128)S(1)} all-to-all(f32[256,8,128]{2,1,0:T(8,128)S(1)} %direction.1), channel_id=1, replica_groups=mesh['shard'=64,'tensor'=4] {'shard','tensor'}, dimensions={0} | all-to-all | bytes 2097152 | tf_op jit(solution)/shard_map/all_to_all | solution.py:187
  51.1 1.3 collective-permute-start
  52.4 1.3 collective-permute-start.1
  53.7 1.3 collective-permute-start.2
  55.0 2.7 %collective-permute-start.3 = (f32[512,512]{1,0:T(8,128)S(1)}, f32[512,512]{1,0:T(8,128)S(1)}, u32[]{:S(2)}, u32[]{:S(2)}) collective-permute-start(f32[512,512]{1,0:T(8,128)S(1)} %bitcast.18), channel_id=1, source_target_pairs={{0,4},{4,0},{2,6},{6,2},{9,13},{13,9},{11,15},{15,11},{16,20},{20,... | collective-permute-start | bytes 3145736 | tf_op jit(solution)/shard_map/ppermute | solution.py:192
  57.8 1.8 %collective-permute-done = f32[176,512]{1,0:T(8,128)S(1)} collective-permute-done((f32[176,512]{1,0:T(8,128)S(1)}, f32[176,512]{1,0:T(8,128)S(1)}, u32[]{:S(2)}, u32[]{:S(2)}) %collective-permute-start) | collective-permute-done | bytes 360480 | tf_op jit(solution)/shard_map/ppermute | solution.py:190
  59.6 1.3 collective-permute-done.1
  60.9 1.0 collective-permute-done.2
  61.8 5.0 %collective-permute-start.4 = (f32[512,512]{1,0:T(8,128)S(1)}, f32[512,512]{1,0:T(8,128)S(1)}, u32[]{:S(2)}, u32[]{:S(2)}) collective-permute-start(f32[512,512]{1,0:T(8,128)S(1)} %constant_dynamic-update-slice_fusion.refs_1_), channel_id=1, source_target_pairs={{0,4},{4,0},{2,6},{6,2},{9,13},{13,9},{11,15},{15,11},{16,20},{20,... | collective-permute-start | bytes 3145736 | tf_op jit(solution)/shard_map/ppermute | solution.py:192
  66.9 2.1 %collective-permute-done.4.refs_3_ = f32[512,512]{1,0:T(8,128)S(1)} collective-permute-done((f32[512,512]{1,0:T(8,128)S(1)}, f32[512,512]{1,0:T(8,128)S(1)}, u32[]{:S(2)}, u32[]{:S(2)}) %collective-permute-start.4) | collective-permute-done | bytes 1048608 | tf_op jit(solution)/shard_map/ppermute | solution.py:192
  68.9 41.1 %newton_schulz.1 = (f32[512,512]{1,0:T(8,128)S(1)}, f32[176,512]{1,0:T(8,128)S(1)}, f32[176,512]{1,0:T(8,128)S(1)}, f32[160,512]{1,0:T(8,128)S(1)}) custom-call(f32[512,512]{1,0:T(8,128)S(1)} %bitcast.19, f32[512,512]{1,0:T(8,128)S(1)} %constant_dynamic-update-slice_fusion.refs_1_, f32[512,512]{1,0:T(8,128)S(1)} %collective-permute-done.3.refs_2_, ...), custom_call_target="tpu_custom_call" | custom-call | tf_op jit(solution)/shard_map/newton_schulz/pallas_call | solution.py:150
  110.0 1.3 collective-permute-start.5
  111.4 1.3 collective-permute-start.6
  112.7 1.3 collective-permute-start.7
  114.0 4.0 %collective-permute-done.7 = f32[160,512]{1,0:T(8,128)S(1)} collective-permute-done((f32[160,512]{1,0:T(8,128)S(1)}, f32[160,512]{1,0:T(8,128)S(1)}, u32[]{:S(2)}, u32[]{:S(2)}) %collective-permute-start.7) | collective-permute-done | bytes 327712 | tf_op jit(solution)/shard_map/ppermute | solution.py:195
  118.0 1.2 maximum_select_fusion
  119.2 8.0 %all-to-all-start.1 = ((f32[256,8,128]{2,1,0:T(8,128)}), f32[256,8,128]{2,1,0:T(8,128)S(1)}, u32[]{:S(2)}, u32[]{:S(2)}) async-start(f32[256,8,128]{2,1,0:T(8,128)} %bitcast.20), calls=%async_computation.1 | async-start | bytes 2097152 | tf_op jit(solution)/shard_map/all_to_all | solution.py:199
  127.1 1.1 convert_add_fusion
  128.3 31.3 %all-to-all-done.1.tiles_ref = f32[256,8,128]{2,1,0:T(8,128)S(1)} async-done(((f32[256,8,128]{2,1,0:T(8,128)}), f32[256,8,128]{2,1,0:T(8,128)S(1)}, u32[]{:S(2)}, u32[]{:S(2)}) %all-to-all-start.1) | async-done | bytes 1048608 | tf_op jit(solution)/shard_map/all_to_all | solution.py:199
  159.5 1.2 place.1
  (13 shorter events, 0.2 us)
Async XLA Ops:
  0.6 1.2 copy-start
  1.9 1.0 copy-start.2
  51.1 8.5 %collective-permute-start = (f32[176,512]{1,0:T(8,128)S(1)}, f32[176,512]{1,0:T(8,128)S(1)}, u32[]{:S(2)}, u32[]{:S(2)}) collective-permute-start(f32[176,512]{1,0:T(8,128)S(1)} %get-tuple-element.11), channel_id=1, source_target_pairs={{3,0},{5,4},{1,2},{7,6},{8,9},{14,13},{10,11},{12,15},{19,16},{21,... | collective-permute-start | bytes 1081352 | tf_op jit(solution)/shard_map/ppermute | solution.py:190
  52.4 8.5 %collective-permute-start.1 = (f32[176,512]{1,0:T(8,128)S(1)}, f32[176,512]{1,0:T(8,128)S(1)}, u32[]{:S(2)}, u32[]{:S(2)}) collective-permute-start(f32[176,512]{1,0:T(8,128)S(1)} %get-tuple-element.10), channel_id=1, source_target_pairs={{192,0},{68,4},{194,2},{70,6},{201,9},{77,13},{203,11},{79,15},{20... | collective-permute-start | bytes 1081352 | tf_op jit(solution)/shard_map/ppermute | solution.py:190
  53.7 8.1 %collective-permute-start.2 = (f32[160,512]{1,0:T(8,128)S(1)}, f32[160,512]{1,0:T(8,128)S(1)}, u32[]{:S(2)}, u32[]{:S(2)}) collective-permute-start(f32[160,512]{1,0:T(8,128)S(1)} %slice_bitcast_fusion.2), channel_id=1, source_target_pairs={{56,0},{12,4},{58,2},{14,6},{1,9},{21,13},{3,11},{23,15},{8,16},{2... | collective-permute-start | bytes 983048 | tf_op jit(solution)/shard_map/ppermute | solution.py:190
  55.0 11.8 %collective-permute-start.3 = (f32[512,512]{1,0:T(8,128)S(1)}, f32[512,512]{1,0:T(8,128)S(1)}, u32[]{:S(2)}, u32[]{:S(2)}) collective-permute-start(f32[512,512]{1,0:T(8,128)S(1)} %bitcast.18), channel_id=1, source_target_pairs={{0,4},{4,0},{2,6},{6,2},{9,13},{13,9},{11,15},{15,11},{16,20},{20,... | collective-permute-start | bytes 3145736 | tf_op jit(solution)/shard_map/ppermute | solution.py:192
  61.8 7.1 %collective-permute-start.4 = (f32[512,512]{1,0:T(8,128)S(1)}, f32[512,512]{1,0:T(8,128)S(1)}, u32[]{:S(2)}, u32[]{:S(2)}) collective-permute-start(f32[512,512]{1,0:T(8,128)S(1)} %constant_dynamic-update-slice_fusion.refs_1_), channel_id=1, source_target_pairs={{0,4},{4,0},{2,6},{6,2},{9,13},{13,9},{11,15},{15,11},{16,20},{20,... | collective-permute-start | bytes 3145736 | tf_op jit(solution)/shard_map/ppermute | solution.py:192
  110.0 7.9 %collective-permute-start.5 = (f32[176,512]{1,0:T(8,128)S(1)}, f32[176,512]{1,0:T(8,128)S(1)}, u32[]{:S(2)}, u32[]{:S(2)}) collective-permute-start(f32[176,512]{1,0:T(8,128)S(1)} %get-tuple-element.7), channel_id=1, source_target_pairs={{0,3},{4,5},{2,1},{6,7},{9,8},{13,14},{11,10},{15,12},{16,19},{20,... | collective-permute-start | bytes 1081352 | tf_op jit(solution)/shard_map/ppermute | solution.py:195
  111.4 6.6 %collective-permute-start.6 = (f32[176,512]{1,0:T(8,128)S(1)}, f32[176,512]{1,0:T(8,128)S(1)}, u32[]{:S(2)}, u32[]{:S(2)}) collective-permute-start(f32[176,512]{1,0:T(8,128)S(1)} %get-tuple-element.8), channel_id=1, source_target_pairs={{0,192},{4,68},{2,194},{6,70},{9,201},{13,77},{11,203},{15,79},{16... | collective-permute-start | bytes 1081352 | tf_op jit(solution)/shard_map/ppermute | solution.py:195
  112.7 5.3 %collective-permute-start.7 = (f32[160,512]{1,0:T(8,128)S(1)}, f32[160,512]{1,0:T(8,128)S(1)}, u32[]{:S(2)}, u32[]{:S(2)}) collective-permute-start(f32[160,512]{1,0:T(8,128)S(1)} %get-tuple-element.9), channel_id=1, source_target_pairs={{0,56},{4,12},{2,58},{6,14},{9,1},{13,21},{11,3},{15,23},{16,8},{2... | collective-permute-start | bytes 983048 | tf_op jit(solution)/shard_map/ppermute | solution.py:195
  119.2 8.0 %copy-start.1 = (f32[64,16,256]{2,1,0:T(8,128)S(1)}, f32[64,16,256]{2,1,0:T(8,128)}, u32[]{:S(2)}) copy-start(f32[64,16,256]{2,1,0:T(8,128)} %momentum_ref.1) | copy-start | bytes 3145732
  119.2 8.0 %copy-start.3 = (bf16[64,16,256]{2,1,0:T(8,128)(2,1)S(1)}, bf16[64,16,256]{2,1,0:T(8,128)(2,1)}, u32[]{:S(2)}) copy-start(bf16[64,16,256]{2,1,0:T(8,128)(2,1)} %gradient_ref.1) | copy-start | bytes 1572868
  119.2 40.4 %all-to-all-start.1 = ((f32[256,8,128]{2,1,0:T(8,128)}), f32[256,8,128]{2,1,0:T(8,128)S(1)}, u32[]{:S(2)}, u32[]{:S(2)}) async-start(f32[256,8,128]{2,1,0:T(8,128)} %bitcast.20), calls=%async_computation.1 | async-start | bytes 2097152 | tf_op jit(solution)/shard_map/all_to_all | solution.py:199
